TPU v7x, 32 devices: a whole 2x2x4 slice. The times are simulated.
32 devices in a mesh: leaf: 8 (over z, y), row: 4 (over x, core).
Axes of the slice: x: 2, y: 2, z: 4, core: 2. Of those that a mesh axis runs over, the one named last changes fastest.
Arguments:
- rhs_blocks: float32 [7, 1024, 256], P(None, 'leaf'), may hold values from -6 to 6
- diag_inverse: float32 [7, 1024, 1024], P(None, 'leaf', 'row'), may hold values from -0.1875 to 0.1875
- lower_blocks: float32 [6, 1024, 1024], P(None, 'leaf', 'row'), may hold values from -0.09375 to 0.09375
- update_rows: int32 [6, 1024], P(None, 'leaf'), may hold values from 512 to 895, as said below
Outputs:
- solution: float32 [7, 1024, 256], P(None, 'leaf')
Inputs may be any that keep to these rules, and one draw needn't show every extreme that they name: update_rows[s, m] = a * 128 + c names column i * 128 + c of an ancestor a of supernode s, where i = m // 128; the 128 entries of one supernode with the same i are distinct.
All inputs are finite; a program needn't handle non-finite values.
Results may differ from a plain program's by a relative error of at most 0.0001.
Values sent between devices are 32-bit elements; how exact they have to be, the bound alone decides.
No kernel may reach another device: no remote copies, remote signals or barrier semaphores. Data moves between devices by JAX's collectives and lax.ppermute only.
A program may use at most 64 MiB of HBM per device.

v0:
```python
import jax
import jax.numpy as jnp
from jax import lax
from jax.sharding import PartitionSpec as P


def local(rhs_blocks, diag_inverse, lower_blocks, update_rows):
    leaf_count = lax.axis_size("leaf")
    node_total = rhs_blocks.shape[0]
    panel_rows = rhs_blocks.shape[1]
    rhs_width = rhs_blocks.shape[2]
    level_total = (node_total + 1).bit_length() - 1
    slice_rows = diag_inverse.shape[2] // leaf_count
    current = rhs_blocks.reshape(node_total * panel_rows, rhs_width)
    stored_slices = [None] * level_total
    for depth_level in range(level_total - 1, -1, -1):
        first_node = 2**level_total - 2 ** (depth_level + 1)
        node_count = 2**depth_level
        stop_node = first_node + node_count
        diag_part = diag_inverse[first_node:stop_node]
        lower_part = lower_blocks[first_node:stop_node] if depth_level > 0 else None
        local_rhs = current[first_node * panel_rows : stop_node * panel_rows].reshape(
            node_count, panel_rows, rhs_width
        )
        partial_value = jnp.einsum(
            "scr,sct->rst", diag_part, local_rhs, precision=lax.Precision.HIGHEST
        )
        complete = lax.psum(partial_value, "leaf")
        stored = lax.dynamic_slice_in_dim(
            complete, lax.axis_index("leaf") * slice_rows, slice_rows, 0
        )
        if depth_level > 0:
            update = jnp.einsum(
                "smr,rst->smt", lower_part, complete, precision=lax.Precision.HIGHEST
            )
        stored_slices[depth_level] = stored
        if depth_level > 0:
            update = lax.psum(update, "row")
            targets = update_rows[first_node:stop_node].reshape(-1)
            current = current.at[targets].add(-update.reshape(-1, rhs_width))
    answer = jnp.zeros((node_total * panel_rows, rhs_width), jnp.float32)
    for depth_level in range(level_total):
        first_node = 2**level_total - 2 ** (depth_level + 1)
        node_count = 2**depth_level
        stop_node = first_node + node_count
        diag_part = diag_inverse[first_node:stop_node]
        residual = stored_slices[depth_level]
        if depth_level > 0:
            lower_part = lower_blocks[first_node:stop_node]
            targets = update_rows[first_node:stop_node].reshape(-1)
            known = answer[targets].reshape(node_count, panel_rows, rhs_width)
            residual = residual - lax.psum_scatter(
                jnp.einsum("smr,smt->rst", lower_part, known, precision=lax.Precision.HIGHEST),
                "leaf",
                scatter_dimension=0,
                tiled=True,
            )
        partial_value = jnp.einsum(
            "scr,rst->sct",
            diag_part,
            lax.all_gather(residual, "leaf", axis=0, tiled=True),
            precision=lax.Precision.HIGHEST,
        )
        solved = lax.psum(partial_value, "row")
        answer = answer.at[first_node * panel_rows : stop_node * panel_rows].set(
            solved.reshape(-1, rhs_width)
        )
    return answer.reshape(node_total, panel_rows, rhs_width)


def solution(mesh):
    placed = (
        P(None, "leaf", None),
        P(None, "leaf", "row"),
        P(None, "leaf", "row"),
        P(None, "leaf"),
    )
    return jax.shard_map(
        local, mesh=mesh, in_specs=placed, out_specs=P(None, "leaf", None), check_vma=False
    )
```

profile of v0, /device:TPU:0, one launch (start us, length us, event | category | flops | bytes accessed | tf_op | source)
XLA Modules:
  0.0 698.2 jit_solution(705623157416841822)
XLA Ops:
  6.5 1.3 copy.104
  8.0 2.0 convolution_bitcast_fusion.1
  10.1 81.5 %all-reduce.14.cloned.1.call-done = f32[256,4,256]{2,0,1:T(8,128)} async-done(((f32[256,4,256]{2,0,1:T(8,128)}), f32[256,4,256]{2,0,1:T(8,128)}) %all-reduce.14.cloned.1.call-update) | async-done | bytes 1048592 | tf_op jit(solution)/shard_map/psum | solution.py:28
  91.6 3.9 convolution_bitcast_fusion.4
  95.6 0.6 slice-done
  96.2 32.2 %all-reduce.16.cloned.1.call-done = f32[4,128,256]{1,2,0:T(8,128)} async-done(((f32[4,128,256]{1,2,0:T(8,128)}), f32[4,128,256]{1,2,0:T(8,128)}) %all-reduce.16.cloned.1.call-update) | async-done | bytes 524304 | tf_op jit(solution)/shard_map/psum | solution.py:38
  128.4 1.9 neg.12
  130.3 1.2 copy.47
  131.6 3.7 scatter_fusion
  135.3 1.4 convolution_bitcast_fusion.3
  136.8 0.6 copy-done.3
  137.4 71.9 %all-reduce.18.cloned.1.call-done = f32[256,2,256]{2,0,1:T(8,128)} async-done(((f32[256,2,256]{2,0,1:T(8,128)}), f32[256,2,256]{2,0,1:T(8,128)}) %all-reduce.18.cloned.1.call-update) | async-done | bytes 524304 | tf_op jit(solution)/shard_map/psum | solution.py:28
  209.3 2.8 convolution_bitcast_fusion.5
  212.1 31.3 %all-reduce.20.cloned.1.call-done = f32[2,128,256]{1,2,0:T(8,128)} async-done(((f32[2,128,256]{1,2,0:T(8,128)}), f32[2,128,256]{1,2,0:T(8,128)}) %all-reduce.20.cloned.1.call-update) | async-done | bytes 262160 | tf_op jit(solution)/shard_map/psum | solution.py:38
  243.5 1.0 neg.14
  244.6 2.3 scatter_fusion.1
  246.9 1.1 convolution_bitcast_fusion.6
  248.1 70.6 %all-reduce.22.cloned.1.call-done = f32[256,1,256]{0,2,1:T(8,128)} async-done(((f32[256,1,256]{0,2,1:T(8,128)}), f32[256,1,256]{0,2,1:T(8,128)}) %all-reduce.22.cloned.1.call-update) | async-done | bytes 262160 | tf_op jit(solution)/shard_map/psum | solution.py:28
  318.8 1.0 constant_dynamic-slice_fusion
  319.8 30.8 %all_gather.9 = f32[256,1,256]{2,1,0:T(1,128)S(1)} all-gather(f32[32,1,256]{2,1,0:T(1,128)S(1)} %copy.52), channel_id=1, replica_groups=mesh['leaf'=8,'row'=4] {'leaf'}, dimensions={0}, use_global_device_ids=true | all-gather | bytes 294912 | tf_op jit(solution)/shard_map/all_gather | solution.py:61
  350.6 1.3 convolution_bitcast_fusion.7
  352.0 30.8 %all-reduce.24.cloned.1.call-done = f32[128,256]{0,1:T(8,128)} async-done(((f32[128,256]{0,1:T(8,128)}), f32[128,256]{0,1:T(8,128)}) %all-reduce.24.cloned.1.call-update) | async-done | bytes 131088 | tf_op jit(solution)/shard_map/psum | solution.py:64
  382.8 1.0 scatter.10
  384.1 1.7 gather_fusion
  385.7 1.6 convolution_bitcast_fusion.2
  387.3 1.0 copy.55
  388.4 0.6 copy-done.4
  389.0 0.6 dynamic-slice.20
  390.3 70.6 %all-reduce.30.cloned.1.call-done = f32[256,2,256]{2,1,0:T(2,128)} async-done(((f32[256,2,256]{2,1,0:T(2,128)}), f32[256,2,256]{2,1,0:T(2,128)}) %all-reduce.30.cloned.1.call-update) | async-done | bytes 524304
  460.9 0.8 constant_dynamic-slice_fusion.2
  461.7 0.8 copy_subtract_fusion.1
  462.6 31.8 %all_gather.10 = f32[256,2,256]{2,1,0:T(2,128)S(1)} all-gather(f32[32,2,256]{2,1,0:T(2,128)S(1)} %copy.57), channel_id=1, replica_groups=mesh['leaf'=8,'row'=4] {'leaf'}, dimensions={0}, use_global_device_ids=true | all-gather | bytes 589824 | tf_op jit(solution)/shard_map/all_gather | solution.py:61
  494.8 0.8 copy.75
  495.8 31.2 %all-reduce.26.cloned.1.call-done = f32[256,256]{0,1:T(8,128)} async-done(((f32[256,256]{0,1:T(8,128)}), f32[256,256]{0,1:T(8,128)}) %all-reduce.26.cloned.1.call-update) | async-done | bytes 262160 | tf_op jit(solution)/shard_map/psum | solution.py:64
  527.0 1.0 constant_dynamic-update-slice_fusion.1
  528.3 1.6 gather_fusion.1
  529.8 2.1 convolution_bitcast_fusion
  531.9 1.3 copy.62
  533.3 78.3 %all-reduce.32.cloned.1.call-done = f32[256,4,256]{2,1,0:T(4,128)} async-done(((f32[256,4,256]{2,1,0:T(4,128)}), f32[256,4,256]{2,1,0:T(4,128)}) %all-reduce.32.cloned.1.call-update) | async-done | bytes 1048592
  611.6 0.9 constant_dynamic-slice_fusion.1
  612.5 0.9 copy_subtract_fusion
  613.5 0.7 copy.64
  614.3 39.8 %all-gather.2.cloned.1.call-done = f32[256,4,256]{2,1,0:T(4,128)} async-done(((f32[32,4,256]{2,1,0:T(4,128)}), f32[256,4,256]{2,1,0:T(4,128)}) %all-gather.2.cloned.1.call-update) | async-done | bytes 1048592 | tf_op jit(solution)/shard_map/all_gather | solution.py:61
  654.1 2.1 fusion
  656.2 1.0 copy.76
  657.3 32.1 %all-reduce.28.cloned.1.call-done = f32[512,256]{0,1:T(8,128)} async-done(((f32[512,256]{0,1:T(8,128)}), f32[512,256]{0,1:T(8,128)}) %all-reduce.28.cloned.1.call-update) | async-done | bytes 524304 | tf_op jit(solution)/shard_map/psum | solution.py:64
  689.3 1.1 constant_dynamic-update-slice_fusion
  690.4 1.2 copy.67
  (43 shorter events, 2.2 us)
Async XLA Ops:
  6.5 1.5 copy-start
  6.5 85.1 %all-reduce.14.cloned.1.call-start = ((), (), s32[]{:S(2)}) async-start(), calls=%async_computation | async-start | bytes 2097152 | tf_op jit(solution)/shard_map/psum | solution.py:28
  10.0 81.6 %copy-start.2 = (f32[6,128,256]{2,1,0:T(8,128)S(1)}, f32[6,128,256]{2,1,0:T(8,128)}, u32[]{:S(2)}) copy-start(f32[6,128,256]{2,1,0:T(8,128)} %param.12) | copy-start | bytes 2359300
  10.1 118.4 %all-reduce.16.cloned.1.call-start = ((), (), s32[]{:S(2)}) async-start(), calls=%async_computation.1 | async-start | bytes 1048576 | tf_op jit(solution)/shard_map/psum | solution.py:38
  95.5 0.7 slice-start
  95.5 113.7 %all-reduce.18.cloned.1.call-start = ((), (), s32[]{:S(2)}) async-start(), calls=%async_computation.2 | async-start | bytes 1048576 | tf_op jit(solution)/shard_map/psum | solution.py:28
  136.7 0.7 copy-start.3
  136.7 106.8 %all-reduce.20.cloned.1.call-start = ((), (), s32[]{:S(2)}) async-start(), calls=%async_computation.3 | async-start | bytes 524288 | tf_op jit(solution)/shard_map/psum | solution.py:38
  212.1 106.7 %all-reduce.22.cloned.1.call-start = ((), (), s32[]{:S(2)}) async-start(), calls=%async_computation.4 | async-start | bytes 524288 | tf_op jit(solution)/shard_map/psum | solution.py:28
  248.0 134.7 %all-reduce.24.cloned.1.call-start = ((), (), s32[]{:S(2)}) async-start(), calls=%async_computation.5 | async-start | bytes 262144 | tf_op jit(solution)/shard_map/psum | solution.py:64
  351.9 108.9 %all-reduce.30.cloned.1.call-start = ((), (), s32[]{:S(2)}) async-start(), calls=%async_computation.9 | async-start | bytes 1048576
  388.3 138.7 %all-reduce.26.cloned.1.call-start = ((), (), s32[]{:S(2)}) async-start(), calls=%async_computation.6 | async-start | bytes 524288 | tf_op jit(solution)/shard_map/psum | solution.py:64
  388.4 0.7 copy-start.4
  495.7 115.9 %all-reduce.32.cloned.1.call-start = ((), (), s32[]{:S(2)}) async-start(), calls=%async_computation.10 | async-start | bytes 2097152
  533.2 120.9 %copy-start.1 = (f32[7,128,256]{2,1,0:T(8,128)S(1)}, f32[7,128,256]{2,1,0:T(8,128)}, u32[]{:S(2)}) copy-start(f32[7,128,256]{2,1,0:T(8,128)} %param.11) | copy-start | bytes 2752516
  533.3 120.9 %all-gather.2.cloned.1.call-start = ((), (), s32[]{:S(2)}) async-start(), calls=%async_computation.7 | async-start | bytes 1179648 | tf_op jit(solution)/shard_map/all_gather | solution.py:61
  614.2 75.1 %all-reduce.28.cloned.1.call-start = ((), (), s32[]{:S(2)}) async-start(), calls=%async_computation.8 | async-start | bytes 1048576 | tf_op jit(solution)/shard_map/psum | solution.py:64
Sparse Core Ops, SparseCore 0:
  10.9 80.7 all-reduce.13
  95.6 32.7 all-reduce.15
  136.8 72.3 all-reduce.17
  212.2 31.2 all-reduce.19
  248.2 70.5 all-reduce.21
  352.0 30.6 all-reduce.23
  388.4 72.3 all-reduce.29
  495.8 31.1 all-reduce.25
  533.4 78.1 all-reduce.31
  614.4 39.7 all-gather.1
  657.4 31.8 all-reduce.27
where the time goes:
time: 699 us; the launch traced here: 698 us
  waiting for transfers between devices  571 us (82%)
  blocking collectives  62.6 us (9%)
  local copies, waits for them, and re-layouts  21.2 us (3%)
  matrix products  18.7 us (3%)
  between operations  14.1 us (2%)
  other arithmetic  10.6 us (2%)
    psum x3, waiting for transfers between devices, local(): complete = lax.psum(partial_value, 'leaf')  224 us
    unnamed x13, waiting for transfers between devices  149 us
    psum x3, waiting for transfers between devices, local(): solved = lax.psum(partial_value, 'row')  94.1 us
    psum x2, waiting for transfers between devices, local(): update = lax.psum(update, 'row')  63.6 us
    all_gather x2, blocking collectives, local(): lax.all_gather(residual, 'leaf', axis=0, tiled=True)  62.6 us
    all_gather x1, waiting for transfers between devices, local(): lax.all_gather(residual, 'leaf', axis=0, tiled=True)  39.8 us
  transfers between devices with their start and end apart: 11, of which 11 were waited for; matrix products, arithmetic and copies ran while one was open for 0% of the time, Pallas kernels for 0%

commit v1 on v0

--- a/solution.py
+++ b/solution.py
@@ -55,12 +55,38 @@
                 scatter_dimension=0,
                 tiled=True,
             )
-        partial_value = jnp.einsum(
+        size, index, span = (lax.axis_size("leaf"), lax.axis_index("leaf"), residual.shape[0])
+        right = [(i, (i + 1) % size) for i in range(size)]
+        downward = [(i, (i - 1) % size) for i in range(size)]
+        middle = size // 2
+        from_left = from_right = residual
+        total = jnp.einsum(
             "scr,rst->sct",
-            diag_part,
-            lax.all_gather(residual, "leaf", axis=0, tiled=True),
+            lax.dynamic_slice_in_dim(diag_part, index * span, residual.shape[0], axis=2),
+            residual,
             precision=lax.Precision.HIGHEST,
         )
+        for step in range(1, middle + 1):
+            from_left = lax.ppermute(from_left, "leaf", right)
+            if step < size - middle:
+                from_right = lax.ppermute(from_right, "leaf", downward)
+                total = total + jnp.einsum(
+                    "scr,rst->sct",
+                    lax.dynamic_slice_in_dim(
+                        diag_part, (index + step) % size * span, from_right.shape[0], axis=2
+                    ),
+                    from_right,
+                    precision=lax.Precision.HIGHEST,
+                )
+            total = total + jnp.einsum(
+                "scr,rst->sct",
+                lax.dynamic_slice_in_dim(
+                    diag_part, (index - step) % size * span, from_left.shape[0], axis=2
+                ),
+                from_left,
+                precision=lax.Precision.HIGHEST,
+            )
+        partial_value = total
         solved = lax.psum(partial_value, "row")
         answer = answer.at[first_node * panel_rows : stop_node * panel_rows].set(
             solved.reshape(-1, rhs_width)

time: 699 us -> 758 us (1.084)
  waiting for transfers between devices: 571 us -> 649 us
  blocking collectives: 62.6 us -> 0 us
  starting transfers between devices: 0.42 us -> 39.4 us
    ppermute x0 -> x21, waiting for transfers between devices: none -> 123 us  [the longest x12 93.5 us: local(): from_left = lax.ppermute(from_left, 'leaf', right)]
    all_gather x2 -> x0, blocking collectives: 62.6 us -> none  [local(): lax.all_gather(residual, 'leaf', axis=0, tiled=True)]
    all_gather x1 -> x0, waiting for transfers between devices: 39.8 us -> none  [local(): lax.all_gather(residual, 'leaf', axis=0, tiled=True)]
    ppermute x0 -> x21, starting transfers between devices: none -> 38.9 us  [the longest x9 28 us: local(): from_right = lax.ppermute(from_right, 'leaf', downward)]
    dot_general x3 -> x24, matrix products: 3.81 us -> 13.3 us  [the longest x12 7.68 us: local(): jnp.einsum('scr,rst->sct', lax.dynamic_slice_in_dim(diag_part, (index - s...]
    unnamed x13 -> x12, waiting for transfers between devices: 149 us -> 149 us
  transfers between devices with their start and end apart: 11 -> 31, of which waited for: 11 -> 24; matrix products, arithmetic and copies ran while one was open for 0% -> 1% of each run, Pallas kernels for 0% -> 0%
where the time goes in v1:
time: 758 us
  waiting for transfers between devices  649 us (86%)
  starting transfers between devices  39.4 us (5%)
  matrix products  25.9 us (3%)
  local copies, waits for them, and re-layouts  18.2 us (2%)
  between operations  14.8 us (2%)
  other arithmetic  10.2 us (1%)
    psum x3, waiting for transfers between devices, local(): complete = lax.psum(partial_value, 'leaf')  224 us
    unnamed x12, waiting for transfers between devices  149 us
    ppermute x12, waiting for transfers between devices, local(): from_left = lax.ppermute(from_left, 'leaf', right)  93.5 us
    psum x3, waiting for transfers between devices, local(): solved = lax.psum(partial_value, 'row')  89.5 us
    psum x2, waiting for transfers between devices, local(): update = lax.psum(update, 'row')  63.6 us
    ppermute x9, waiting for transfers between devices, local(): from_right = lax.ppermute(from_right, 'leaf', downward)  29.7 us
    ppermute x9, starting transfers between devices, local(): from_right = lax.ppermute(from_right, 'leaf', downward)  28 us
  transfers between devices with their start and end apart: 31, of which 24 were waited for; matrix products, arithmetic and copies ran while one was open for 1% of the time, Pallas kernels for 0%

profile of v1, /device:TPU:0, one launch (start us, length us, event | category | flops | bytes accessed | tf_op | source)
XLA Modules:
  0.0 757.6 jit_solution(8676655858397974763)
XLA Ops:
  6.5 1.3 copy.171
  8.0 2.0 convolution_bitcast_fusion.1
  10.1 81.6 %all-reduce.14.cloned.1.call-done = f32[256,4,256]{0,2,1:T(8,128)} async-done(((f32[256,4,256]{0,2,1:T(8,128)}), f32[256,4,256]{0,2,1:T(8,128)}) %all-reduce.14.cloned.1.call-update) | async-done | bytes 1048592 | tf_op jit(solution)/shard_map/psum | solution.py:28
  91.6 3.1 convolution_bitcast_fusion.4
  95.4 32.2 %all-reduce.16.cloned.1.call-done = f32[4,128,256]{1,2,0:T(8,128)} async-done(((f32[4,128,256]{1,2,0:T(8,128)}), f32[4,128,256]{1,2,0:T(8,128)}) %all-reduce.16.cloned.1.call-update) | async-done | bytes 524304 | tf_op jit(solution)/shard_map/psum | solution.py:38
  127.7 1.9 neg.12
  130.8 3.7 scatter_fusion
  134.5 1.4 convolution_bitcast_fusion.3
  136.6 71.9 %all-reduce.18.cloned.1.call-done = f32[256,2,256]{0,2,1:T(8,128)} async-done(((f32[256,2,256]{0,2,1:T(8,128)}), f32[256,2,256]{0,2,1:T(8,128)}) %all-reduce.18.cloned.1.call-update) | async-done | bytes 524304 | tf_op jit(solution)/shard_map/psum | solution.py:28
  208.5 2.3 convolution_bitcast_fusion.5
  210.9 31.3 %all-reduce.20.cloned.1.call-done = f32[2,128,256]{1,2,0:T(8,128)} async-done(((f32[2,128,256]{1,2,0:T(8,128)}), f32[2,128,256]{1,2,0:T(8,128)}) %all-reduce.20.cloned.1.call-update) | async-done | bytes 262160 | tf_op jit(solution)/shard_map/psum | solution.py:38
  243.4 2.3 scatter_fusion.1
  247.0 70.5 %all-reduce.22.cloned.1.call-done = f32[256,1,256]{0,2,1:T(8,128)} async-done(((f32[256,1,256]{0,2,1:T(8,128)}), f32[256,1,256]{0,2,1:T(8,128)}) %all-reduce.22.cloned.1.call-update) | async-done | bytes 262160 | tf_op jit(solution)/shard_map/psum | solution.py:28
  318.6 2.6 collective-permute-start
  321.6 7.4 collective-permute-done.1
  329.0 4.7 collective-permute-start.2
  334.4 2.4 collective-permute-done.3
  337.9 4.0 collective-permute-start.4
  342.2 3.0 collective-permute-done.5
  345.9 7.0 collective-permute-done.6
  354.1 28.5 %all-reduce.24.cloned.1.call-done = f32[128,256]{1,0:T(8,128)} async-done(((f32[128,256]{1,0:T(8,128)}), f32[128,256]{1,0:T(8,128)}) %all-reduce.24.cloned.1.call-update) | async-done | bytes 131088 | tf_op jit(solution)/shard_map/psum | solution.py:90
  388.3 70.5 %all-reduce.30.cloned.1.call-done = f32[256,2,256]{2,1,0:T(2,128)} async-done(((f32[256,2,256]{2,1,0:T(2,128)}), f32[256,2,256]{2,1,0:T(2,128)}) %all-reduce.30.cloned.1.call-update) | async-done | bytes 524304
  459.9 2.7 collective-permute-start.7
  463.0 9.0 %collective-permute-done.7 = f32[32,2,256]{0,2,1:T(8,128)S(1)} collective-permute-done((f32[32,2,256]{0,2,1:T(8,128)S(1)}, f32[32,2,256]{0,2,1:T(8,128)S(1)}, u32[]{:S(2)}, u32[]{:S(2)}) %collective-permute-start.7) | collective-permute-done | bytes 65568 | tf_op jit(solution)/shard_map/ppermute | solution.py:72
  473.5 3.4 collective-permute-done.8
  476.9 2.4 collective-permute-start.10
  479.8 7.9 %collective-permute-done.10 = f32[32,2,256]{0,2,1:T(8,128)S(1)} collective-permute-done((f32[32,2,256]{0,2,1:T(8,128)S(1)}, f32[32,2,256]{0,2,1:T(8,128)S(1)}, u32[]{:S(2)}, u32[]{:S(2)}) %collective-permute-start.10) | collective-permute-done | bytes 65568 | tf_op jit(solution)/shard_map/ppermute | solution.py:70
  488.2 4.7 collective-permute-start.11
  493.3 5.4 collective-permute-done.12
  499.2 2.5 collective-permute-start.13
  502.2 6.3 collective-permute-done.13
  509.7 30.4 %all-reduce.26.cloned.1.call-done = f32[256,256]{1,0:T(8,128)} async-done(((f32[256,256]{1,0:T(8,128)}), f32[256,256]{1,0:T(8,128)}) %all-reduce.26.cloned.1.call-update) | async-done | bytes 262160 | tf_op jit(solution)/shard_map/psum | solution.py:90
  541.1 1.6 gather_fusion.1
  542.7 2.1 convolution_bitcast_fusion
  544.8 1.3 copy.102
  546.2 78.2 %all-reduce.32.cloned.1.call-done = f32[256,4,256]{2,1,0:T(4,128)} async-done(((f32[256,4,256]{2,1,0:T(4,128)}), f32[256,4,256]{2,1,0:T(4,128)}) %all-reduce.32.cloned.1.call-update) | async-done | bytes 1048592
  626.3 1.2 dynamic-slice_subtract_fusion
  627.6 3.0 collective-permute-start.14
  631.2 20.6 %collective-permute-done.14 = f32[32,4,256]{0,2,1:T(8,128)S(1)} collective-permute-done((f32[32,4,256]{0,2,1:T(8,128)S(1)}, f32[32,4,256]{0,2,1:T(8,128)S(1)}, u32[]{:S(2)}, u32[]{:S(2)}) %collective-permute-start.14) | collective-permute-done | bytes 131104 | tf_op jit(solution)/shard_map/ppermute | solution.py:72
  653.1 10.0 %collective-permute-done.15 = f32[32,4,256]{0,2,1:T(8,128)S(1)} collective-permute-done((f32[32,4,256]{0,2,1:T(8,128)S(1)}, f32[32,4,256]{0,2,1:T(8,128)S(1)}, u32[]{:S(2)}, u32[]{:S(2)}) %collective-permute-start.15) | collective-permute-done | bytes 131104 | tf_op jit(solution)/shard_map/ppermute | solution.py:70
  663.1 2.5 collective-permute-start.17
  666.3 13.4 %collective-permute-done.17 = f32[32,4,256]{0,2,1:T(8,128)S(1)} collective-permute-done((f32[32,4,256]{0,2,1:T(8,128)S(1)}, f32[32,4,256]{0,2,1:T(8,128)S(1)}, u32[]{:S(2)}, u32[]{:S(2)}) %collective-permute-start.17) | collective-permute-done | bytes 131104 | tf_op jit(solution)/shard_map/ppermute | solution.py:70
  680.3 4.8 collective-permute-start.18
  685.7 16.0 %collective-permute-done.19 = f32[32,4,256]{0,2,1:T(8,128)S(1)} collective-permute-done((f32[32,4,256]{0,2,1:T(8,128)S(1)}, f32[32,4,256]{0,2,1:T(8,128)S(1)}, u32[]{:S(2)}, u32[]{:S(2)}) %collective-permute-start.19) | collective-permute-done | bytes 131104 | tf_op jit(solution)/shard_map/ppermute | solution.py:70
  701.7 2.5 collective-permute-start.20
  705.5 11.3 %collective-permute-done.20 = f32[32,4,256]{0,2,1:T(8,128)S(1)} collective-permute-done((f32[32,4,256]{0,2,1:T(8,128)S(1)}, f32[32,4,256]{0,2,1:T(8,128)S(1)}, u32[]{:S(2)}, u32[]{:S(2)}) %collective-permute-start.20) | collective-permute-done | bytes 131104 | tf_op jit(solution)/shard_map/ppermute | solution.py:70
  716.8 1.4 convolution_add_fusion
  718.2 30.5 %all-reduce.28.cloned.1.call-done = f32[512,256]{1,0:T(8,128)} async-done(((f32[512,256]{1,0:T(8,128)}), f32[512,256]{1,0:T(8,128)}) %all-reduce.28.cloned.1.call-update) | async-done | bytes 524304 | tf_op jit(solution)/shard_map/psum | solution.py:90
  (104 shorter events, 32.0 us)
Async XLA Ops:
  6.5 1.5 copy-start.1
  6.5 85.1 %all-reduce.14.cloned.1.call-start = ((), (), s32[]{:S(2)}) async-start(), calls=%async_computation | async-start | bytes 2097152 | tf_op jit(solution)/shard_map/psum | solution.py:28
  10.0 81.6 %copy-start.2 = (f32[6,128,256]{2,1,0:T(8,128)S(1)}, f32[6,128,256]{2,1,0:T(8,128)}, u32[]{:S(2)}) copy-start(f32[6,128,256]{2,1,0:T(8,128)} %param.12) | copy-start | bytes 2359300
  10.0 117.6 %all-reduce.16.cloned.1.call-start = ((), (), s32[]{:S(2)}) async-start(), calls=%async_computation.1 | async-start | bytes 1048576 | tf_op jit(solution)/shard_map/psum | solution.py:38
  94.7 0.7 slice-start
  94.7 113.7 %all-reduce.18.cloned.1.call-start = ((), (), s32[]{:S(2)}) async-start(), calls=%async_computation.2 | async-start | bytes 1048576 | tf_op jit(solution)/shard_map/psum | solution.py:28
  135.9 0.7 copy-start.6
  135.9 106.3 %all-reduce.20.cloned.1.call-start = ((), (), s32[]{:S(2)}) async-start(), calls=%async_computation.3 | async-start | bytes 524288 | tf_op jit(solution)/shard_map/psum | solution.py:38
  210.8 106.7 %all-reduce.22.cloned.1.call-start = ((), (), s32[]{:S(2)}) async-start(), calls=%async_computation.4 | async-start | bytes 524288 | tf_op jit(solution)/shard_map/psum | solution.py:28
  246.8 135.8 %all-reduce.24.cloned.1.call-start = ((), (), s32[]{:S(2)}) async-start(), calls=%async_computation.5 | async-start | bytes 262144 | tf_op jit(solution)/shard_map/psum | solution.py:90
  317.5 3.7 copy-start.5
  318.6 10.4 %collective-permute-start = (f32[32,1,256]{0,2,1:T(8,128)S(1)}, f32[32,1,256]{0,2,1:T(8,128)S(1)}, u32[]{:S(2)}, u32[]{:S(2)}) collective-permute-start(f32[32,1,256]{0,2,1:T(8,128)S(1)} %constant_dynamic-slice_fusion), channel_id=1, source_target_pairs={{0,28},{4,0},{8,4},{12,8},{16,12},{20,16},{24,20},{28,24},{1,29},{... | collective-permute-start | bytes 98312 | tf_op jit(solution)/shard_map/ppermute | solution.py:72
  321.2 7.8 %collective-permute-start.1 = (f32[32,1,256]{0,2,1:T(8,128)S(1)}, f32[32,1,256]{0,2,1:T(8,128)S(1)}, u32[]{:S(2)}, u32[]{:S(2)}) collective-permute-start(f32[32,1,256]{0,2,1:T(8,128)S(1)} %constant_dynamic-slice_fusion), channel_id=1, source_target_pairs={{0,4},{4,8},{8,12},{12,16},{16,20},{20,24},{24,28},{28,0},{1,5},{5... | collective-permute-start | bytes 98312 | tf_op jit(solution)/shard_map/ppermute | solution.py:70
  329.0 7.8 %collective-permute-start.3 = (f32[32,1,256]{0,2,1:T(8,128)S(1)}, f32[32,1,256]{0,2,1:T(8,128)S(1)}, u32[]{:S(2)}, u32[]{:S(2)}) collective-permute-start(f32[32,1,256]{0,2,1:T(8,128)S(1)} %collective-permute-done.1), channel_id=1, source_target_pairs={{0,4},{4,8},{8,12},{12,16},{16,20},{20,24},{24,28},{28,0},{1,5},{5... | collective-permute-start | bytes 98312 | tf_op jit(solution)/shard_map/ppermute | solution.py:70
  329.0 8.9 %collective-permute-start.2 = (f32[32,1,256]{0,2,1:T(8,128)S(1)}, f32[32,1,256]{0,2,1:T(8,128)S(1)}, u32[]{:S(2)}, u32[]{:S(2)}) collective-permute-start(f32[32,1,256]{0,2,1:T(8,128)S(1)} %collective-permute-done), channel_id=1, source_target_pairs={{0,28},{4,0},{8,4},{12,8},{16,12},{20,16},{24,20},{28,24},{1,29},{... | collective-permute-start | bytes 98312 | tf_op jit(solution)/shard_map/ppermute | solution.py:72
  336.8 8.4 %collective-permute-start.5 = (f32[32,1,256]{0,2,1:T(8,128)S(1)}, f32[32,1,256]{0,2,1:T(8,128)S(1)}, u32[]{:S(2)}, u32[]{:S(2)}) collective-permute-start(f32[32,1,256]{0,2,1:T(8,128)S(1)} %collective-permute-done.3), channel_id=1, source_target_pairs={{0,4},{4,8},{8,12},{12,16},{16,20},{20,24},{24,28},{28,0},{1,5},{5... | collective-permute-start | bytes 98312 | tf_op jit(solution)/shard_map/ppermute | solution.py:70
  337.9 7.7 %collective-permute-start.4 = (f32[32,1,256]{0,2,1:T(8,128)S(1)}, f32[32,1,256]{0,2,1:T(8,128)S(1)}, u32[]{:S(2)}, u32[]{:S(2)}) collective-permute-start(f32[32,1,256]{0,2,1:T(8,128)S(1)} %collective-permute-done.2), channel_id=1, source_target_pairs={{0,28},{4,0},{8,4},{12,8},{16,12},{20,16},{24,20},{28,24},{1,29},{... | collective-permute-start | bytes 98312 | tf_op jit(solution)/shard_map/ppermute | solution.py:72
  345.2 7.7 %collective-permute-start.6 = (f32[32,1,256]{0,2,1:T(8,128)S(1)}, f32[32,1,256]{0,2,1:T(8,128)S(1)}, u32[]{:S(2)}, u32[]{:S(2)}) collective-permute-start(f32[32,1,256]{0,2,1:T(8,128)S(1)} %collective-permute-done.5), channel_id=1, source_target_pairs={{0,4},{4,8},{8,12},{12,16},{16,20},{20,24},{24,28},{28,0},{1,5},{5... | collective-permute-start | bytes 98312 | tf_op jit(solution)/shard_map/ppermute | solution.py:70
  353.9 104.9 %all-reduce.30.cloned.1.call-start = ((), (), s32[]{:S(2)}) async-start(), calls=%async_computation.8 | async-start | bytes 1048576
  386.2 73.5 %copy-start.4 = (f32[256,2,256]{0,2,1:T(8,128)S(1)}, f32[256,2,256]{0,2,1:T(8,128)}, u32[]{:S(2)}) copy-start(f32[256,2,256]{0,2,1:T(8,128)} %all-reduce.18.cloned.1.call-done) | copy-start | bytes 1572868
  386.3 153.9 %all-reduce.26.cloned.1.call-start = ((), (), s32[]{:S(2)}) async-start(), calls=%async_computation.6 | async-start | bytes 524288 | tf_op jit(solution)/shard_map/psum | solution.py:90
  386.3 0.7 copy-start.7
  459.9 12.2 %collective-permute-start.7 = (f32[32,2,256]{0,2,1:T(8,128)S(1)}, f32[32,2,256]{0,2,1:T(8,128)S(1)}, u32[]{:S(2)}, u32[]{:S(2)}) collective-permute-start(f32[32,2,256]{0,2,1:T(8,128)S(1)} %dynamic-slice_subtract_fusion.1), channel_id=1, source_target_pairs={{0,28},{4,0},{8,4},{12,8},{16,12},{20,16},{24,20},{28,24},{1,29},{... | collective-permute-start | bytes 196616 | tf_op jit(solution)/shard_map/ppermute | solution.py:72
  462.6 14.3 %collective-permute-start.8 = (f32[32,2,256]{0,2,1:T(8,128)S(1)}, f32[32,2,256]{0,2,1:T(8,128)S(1)}, u32[]{:S(2)}, u32[]{:S(2)}) collective-permute-start(f32[32,2,256]{0,2,1:T(8,128)S(1)} %dynamic-slice_subtract_fusion.1), channel_id=1, source_target_pairs={{0,4},{4,8},{8,12},{12,16},{16,20},{20,24},{24,28},{28,0},{1,5},{5... | collective-permute-start | bytes 196616 | tf_op jit(solution)/shard_map/ppermute | solution.py:70
  472.1 16.1 %collective-permute-start.9 = (f32[32,2,256]{0,2,1:T(8,128)S(1)}, f32[32,2,256]{0,2,1:T(8,128)S(1)}, u32[]{:S(2)}, u32[]{:S(2)}) collective-permute-start(f32[32,2,256]{0,2,1:T(8,128)S(1)} %collective-permute-done.7), channel_id=1, source_target_pairs={{0,28},{4,0},{8,4},{12,8},{16,12},{20,16},{24,20},{28,24},{1,29},{... | collective-permute-start | bytes 196616 | tf_op jit(solution)/shard_map/ppermute | solution.py:72
  476.9 10.8 %collective-permute-start.10 = (f32[32,2,256]{0,2,1:T(8,128)S(1)}, f32[32,2,256]{0,2,1:T(8,128)S(1)}, u32[]{:S(2)}, u32[]{:S(2)}) collective-permute-start(f32[32,2,256]{0,2,1:T(8,128)S(1)} %collective-permute-done.8), channel_id=1, source_target_pairs={{0,4},{4,8},{8,12},{12,16},{16,20},{20,24},{24,28},{28,0},{1,5},{5... | collective-permute-start | bytes 196616 | tf_op jit(solution)/shard_map/ppermute | solution.py:70
  488.1 10.7 %collective-permute-start.12 = (f32[32,2,256]{0,2,1:T(8,128)S(1)}, f32[32,2,256]{0,2,1:T(8,128)S(1)}, u32[]{:S(2)}, u32[]{:S(2)}) collective-permute-start(f32[32,2,256]{0,2,1:T(8,128)S(1)} %collective-permute-done.10), channel_id=1, source_target_pairs={{0,4},{4,8},{8,12},{12,16},{16,20},{20,24},{24,28},{28,0},{1,5},{5... | collective-permute-start | bytes 196616 | tf_op jit(solution)/shard_map/ppermute | solution.py:70
  488.2 13.5 %collective-permute-start.11 = (f32[32,2,256]{0,2,1:T(8,128)S(1)}, f32[32,2,256]{0,2,1:T(8,128)S(1)}, u32[]{:S(2)}, u32[]{:S(2)}) collective-permute-start(f32[32,2,256]{0,2,1:T(8,128)S(1)} %collective-permute-done.9), channel_id=1, source_target_pairs={{0,28},{4,0},{8,4},{12,8},{16,12},{20,16},{24,20},{28,24},{1,29},{... | collective-permute-start | bytes 196616 | tf_op jit(solution)/shard_map/ppermute | solution.py:72
  499.2 9.3 %collective-permute-start.13 = (f32[32,2,256]{0,2,1:T(8,128)S(1)}, f32[32,2,256]{0,2,1:T(8,128)S(1)}, u32[]{:S(2)}, u32[]{:S(2)}) collective-permute-start(f32[32,2,256]{0,2,1:T(8,128)S(1)} %collective-permute-done.12), channel_id=1, source_target_pairs={{0,4},{4,8},{8,12},{12,16},{16,20},{20,24},{24,28},{28,0},{1,5},{5... | collective-permute-start | bytes 196616 | tf_op jit(solution)/shard_map/ppermute | solution.py:70
  509.6 114.8 %all-reduce.32.cloned.1.call-start = ((), (), s32[]{:S(2)}) async-start(), calls=%async_computation.9 | async-start | bytes 2097152
  546.1 80.2 %copy-start.3 = (f32[256,4,256]{0,2,1:T(8,128)S(1)}, f32[256,4,256]{0,2,1:T(8,128)}, u32[]{:S(2)}) copy-start(f32[256,4,256]{0,2,1:T(8,128)} %all-reduce.14.cloned.1.call-done) | copy-start | bytes 3145732
  546.1 202.6 %all-reduce.28.cloned.1.call-start = ((), (), s32[]{:S(2)}) async-start(), calls=%async_computation.7 | async-start | bytes 1048576 | tf_op jit(solution)/shard_map/psum | solution.py:90
  627.6 24.3 %collective-permute-start.14 = (f32[32,4,256]{0,2,1:T(8,128)S(1)}, f32[32,4,256]{0,2,1:T(8,128)S(1)}, u32[]{:S(2)}, u32[]{:S(2)}) collective-permute-start(f32[32,4,256]{0,2,1:T(8,128)S(1)} %dynamic-slice_subtract_fusion), channel_id=1, source_target_pairs={{0,28},{4,0},{8,4},{12,8},{16,12},{20,16},{24,20},{28,24},{1,29},{... | collective-permute-start | bytes 393224 | tf_op jit(solution)/shard_map/ppermute | solution.py:72
  630.6 32.5 %collective-permute-start.15 = (f32[32,4,256]{0,2,1:T(8,128)S(1)}, f32[32,4,256]{0,2,1:T(8,128)S(1)}, u32[]{:S(2)}, u32[]{:S(2)}) collective-permute-start(f32[32,4,256]{0,2,1:T(8,128)S(1)} %dynamic-slice_subtract_fusion), channel_id=1, source_target_pairs={{0,4},{4,8},{8,12},{12,16},{16,20},{20,24},{24,28},{28,0},{1,5},{5... | collective-permute-start | bytes 393224 | tf_op jit(solution)/shard_map/ppermute | solution.py:70
  651.9 28.4 %collective-permute-start.16 = (f32[32,4,256]{0,2,1:T(8,128)S(1)}, f32[32,4,256]{0,2,1:T(8,128)S(1)}, u32[]{:S(2)}, u32[]{:S(2)}) collective-permute-start(f32[32,4,256]{0,2,1:T(8,128)S(1)} %collective-permute-done.14), channel_id=1, source_target_pairs={{0,28},{4,0},{8,4},{12,8},{16,12},{20,16},{24,20},{28,24},{1,29},{... | collective-permute-start | bytes 393224 | tf_op jit(solution)/shard_map/ppermute | solution.py:72
  663.1 16.5 %collective-permute-start.17 = (f32[32,4,256]{0,2,1:T(8,128)S(1)}, f32[32,4,256]{0,2,1:T(8,128)S(1)}, u32[]{:S(2)}, u32[]{:S(2)}) collective-permute-start(f32[32,4,256]{0,2,1:T(8,128)S(1)} %collective-permute-done.15), channel_id=1, source_target_pairs={{0,4},{4,8},{8,12},{12,16},{16,20},{20,24},{24,28},{28,0},{1,5},{5... | collective-permute-start | bytes 393224 | tf_op jit(solution)/shard_map/ppermute | solution.py:70
  679.7 22.0 %collective-permute-start.19 = (f32[32,4,256]{0,2,1:T(8,128)S(1)}, f32[32,4,256]{0,2,1:T(8,128)S(1)}, u32[]{:S(2)}, u32[]{:S(2)}) collective-permute-start(f32[32,4,256]{0,2,1:T(8,128)S(1)} %collective-permute-done.17), channel_id=1, source_target_pairs={{0,4},{4,8},{8,12},{12,16},{16,20},{20,24},{24,28},{28,0},{1,5},{5... | collective-permute-start | bytes 393224 | tf_op jit(solution)/shard_map/ppermute | solution.py:70
  680.3 24.5 %collective-permute-start.18 = (f32[32,4,256]{0,2,1:T(8,128)S(1)}, f32[32,4,256]{0,2,1:T(8,128)S(1)}, u32[]{:S(2)}, u32[]{:S(2)}) collective-permute-start(f32[32,4,256]{0,2,1:T(8,128)S(1)} %collective-permute-done.16), channel_id=1, source_target_pairs={{0,28},{4,0},{8,4},{12,8},{16,12},{20,16},{24,20},{28,24},{1,29},{... | collective-permute-start | bytes 393224 | tf_op jit(solution)/shard_map/ppermute | solution.py:72
  701.7 15.1 %collective-permute-start.20 = (f32[32,4,256]{0,2,1:T(8,128)S(1)}, f32[32,4,256]{0,2,1:T(8,128)S(1)}, u32[]{:S(2)}, u32[]{:S(2)}) collective-permute-start(f32[32,4,256]{0,2,1:T(8,128)S(1)} %collective-permute-done.19), channel_id=1, source_target_pairs={{0,4},{4,8},{8,12},{12,16},{16,20},{20,24},{24,28},{28,0},{1,5},{5... | collective-permute-start | bytes 393224 | tf_op jit(solution)/shard_map/ppermute | solution.py:70
  749.8 0.9 copy-start
Sparse Core Ops, SparseCore 0:
  10.9 80.7 all-reduce.13
  94.8 32.7 all-reduce.15
  136.0 72.3 all-reduce.17
  211.0 31.2 all-reduce.19
  246.9 70.5 all-reduce.21
  354.0 28.6 all-reduce.23
  386.5 72.2 all-reduce.29
  509.8 30.3 all-reduce.25
  546.2 78.1 all-reduce.31
  718.3 30.3 all-reduce.27
